TPU v7x, 32 devices: a whole 2x2x4 slice. The times are simulated.
32 devices in a mesh: rows: 8 (over y, x, core), loop: 4 (over z).
Axes of the slice: x: 2, y: 2, z: 4, core: 2. Of those that a mesh axis runs over, the one named last changes fastest.
Arguments:
- integrals: float32 [2, 2, 8192, 8192], P(None, None, 'rows', 'loop'), may hold values from -6 to 6
- mask: int32 [2, 64, 64], P(None, 'rows', 'loop'), may hold values 0 or 1
- coeffs: float32 [8192, 640], P('loop'), may hold values from -0.0625 to 0.0625
Outputs:
- exchange: float32 [8192, 8192], P('rows', 'loop')
All inputs are finite; a program needn't handle non-finite values. No bound on the sum of `mask` on one device may be relied on, other than what follows from the above.
Results may differ from a plain program's by a relative error of at most 0.00009.
Values sent between devices are 32-bit elements; how exact they have to be, the bound alone decides.
A program may use at most 192 MiB of HBM per device.

v0:
```python
import functools

import jax
import jax.numpy as jnp
from jax import lax
from jax.experimental import pallas as pl
from jax.experimental.pallas import tpu as pltpu
from jax.sharding import PartitionSpec as P

TILE = 128
CHUNK = 32
GROUP = 8
HOP = 2
REACH = 2
SLOTS = 8
MESH = pl.DeviceIdType.MESH


def split(x):
    high = x.astype(jnp.bfloat16)
    low = (x - high.astype(jnp.float32)).astype(jnp.bfloat16)
    return high, low


def ring_place(pair, pairs):
    if pairs == 4:
        return pair + (pair // 2) * (1 - 2 * lax.rem(pair, 2))
    return pair


def exchange_kernel(
    loops, row_count, scale, integrals_ref, mask_ref, coeffs_ref, out_ref,
    own, pin, sin, cols, left, high_ref, low_ref, tile, spare, tile_sem, coeffs_sem,
    up_send, up_recv, dn_send, dn_recv, ch_send, ch_recv, pt_send, pt_recv,
):
    depth, mrows = own.shape
    naux, lcols = integrals_ref.shape[1], integrals_ref.shape[3]
    norbit = coeffs_ref.shape[1]
    ring = pin.shape[0] // CHUNK
    wide = tile.shape[1]
    tiles = mrows // wide
    tile_count = integrals_ref.shape[0] * naux * tiles
    count = depth // CHUNK
    span = CHUNK * GROUP
    pairs = row_count // 2
    r, l = lax.axis_index("rows"), lax.axis_index("loop")
    pair, core = r // 2, lax.rem(r, 2)
    partner = r + 1 - 2 * core
    turn = 1 - 2 * core
    place = ring_place(pair, pairs)
    far = lax.rem((place - ring_place(l, pairs)) * turn + pairs, pairs)
    ahead = ring_place(lax.rem(place + turn + pairs, pairs), pairs) * 2 + core
    behind = ring_place(lax.rem(place - turn + pairs, pairs), pairs) * 2 + core

    def fetch(u):
        part, m = u // tiles, lax.rem(u, tiles)
        return pltpu.make_async_copy(
            integrals_ref.at[
                part // naux, lax.rem(part, naux), pl.ds(pl.multiple_of(m * wide, wide), wide), :
            ],
            tile.at[lax.rem(u, 2)],
            tile_sem.at[lax.rem(u, 2)],
        )

    def half(u):
        part, m = u // tiles, lax.rem(u, tiles)
        fetch(u).wait()
        blocks = tile[lax.rem(u, 2)].reshape(wide // TILE, TILE, lcols)
        mask = mask_ref[part // naux, m][:, None, :]
        high, low = split((blocks * mask).reshape(wide, lcols))

        def times(a, b):
            return lax.dot_general(
                a, b, (((1,), (1,)), ((), ())), preferred_element_type=jnp.float32
            )

        value = times(high_ref[...], high) + times(high_ref[...], low) + times(low_ref[...], high)
        at = pl.ds(pl.multiple_of(part * norbit, norbit), norbit)
        own[at, pl.ds(pl.multiple_of(m * wide, wide), wide)] = value

        @pl.when(u + 2 < tile_count)
        def _():
            fetch(u + 2).start()

    room = spare if spare.shape == coeffs_ref.shape else cols.at[0, pl.ds(0, lcols), pl.ds(0, norbit)]
    load = pltpu.make_async_copy(coeffs_ref, room, coeffs_sem)
    load.start()
    fetch(0).start()
    fetch(1).start()
    load.wait()

    @pl.loop(0, lcols // 256)
    def _(n):
        at = pl.ds(pl.multiple_of(n * 256, 256), 256)
        high_ref[:, at], low_ref[:, at] = split(room[at, :].T)

    barrier = pltpu.get_barrier_semaphore()
    for other in (partner, ahead, behind):
        pl.semaphore_signal(barrier, inc=1, device_id={"rows": other}, device_id_type=MESH)

    @pl.when(l > 0)
    def _():
        pl.semaphore_signal(barrier, inc=1, device_id={"loop": l - 1}, device_id_type=MESH)

    @pl.when(l < loops - 1)
    def _():
        pl.semaphore_signal(barrier, inc=1, device_id={"loop": l + 1}, device_id_type=MESH)

    neighbours = jnp.where(l > 0, 1, 0) + jnp.where(l < loops - 1, 1, 0)
    pl.semaphore_wait(barrier, 3 + neighbours)

    @pl.loop(0, tiles)
    def _(u):
        half(u)

    pace = max(norbit // CHUNK // tiles, 1)

    def rows_of(j):
        return pl.ds(pl.multiple_of(j * CHUNK, CHUNK), CHUNK)

    def slot_of(j):
        return pl.ds(pl.multiple_of(lax.rem(j, ring) * CHUNK, CHUNK), CHUNK)

    def copy(src, dst, send, recv, j, target):
        return pltpu.make_async_remote_copy(
            src_ref=src, dst_ref=dst, send_sem=send.at[lax.rem(j, SLOTS)], recv_sem=recv.at[j],
            device_id=target, device_id_type=MESH,
        )

    def up(j):
        return copy(pin.at[slot_of(j)], pin.at[slot_of(j)], up_send, up_recv, j, {"loop": l + 1})

    def down(j):
        return copy(sin.at[slot_of(j)], sin.at[slot_of(j)], dn_send, dn_recv, j, {"loop": l - 1})

    def chain(j):
        ref = cols.at[core, rows_of(j)]
        return copy(ref, ref, ch_send, ch_recv, j, {"rows": ahead})

    def share(j):
        ref = cols.at[core, rows_of(j)]
        return copy(ref, ref, pt_send, pt_recv, j, {"rows": partner})

    def taken(j):
        ref = cols.at[1 - core, rows_of(j)]
        return copy(ref, ref, pt_send, pt_recv, j, {"rows": partner})

    def send(make, j):
        @pl.when(j >= SLOTS)
        def _():
            make(j - SLOTS).wait_send()

        make(j).start()

    def line(held, make, j, first, last):
        @pl.when((j >= 0) & (j < count))
        def _():
            at, slot = rows_of(j), slot_of(j)

            @pl.when(first)
            def _():
                held[slot, :] = own[at, :]

            @pl.when(jnp.logical_not(first))
            def _():
                make(j).wait_recv()
                held[slot, :] = held[slot, :] + own[at, :]

            @pl.when(jnp.logical_not(last))
            def _():
                send(make, j)

    settle = HOP * jnp.maximum(l, loops - 1 - l)

    def multiply(g, n):
        at = pl.ds(pl.multiple_of(g * span, span), span)

        @pl.when(n == 0)
        def _():
            @pl.loop(0, mrows // 256)
            def _(m):
                mine = pl.ds(pl.multiple_of(m * 256, 256), 256)
                high, low = split(own[at, mine].T)
                left[mine, pl.ds(0, span)] = high
                left[mine, pl.ds(span, span)] = high
                left[mine, pl.ds(2 * span, span)] = low

        @pl.when(n < 2 * (mrows // 256))
        def _():
            block = n // (mrows // 256)
            inner = pl.multiple_of(lax.rem(n, mrows // 256) * 256, 256)
            high, low = split(cols[block, at, pl.ds(inner, 256)])
            right = jnp.concatenate([high, low, high], axis=0)
            theirs = pl.ds(pl.multiple_of(n * 256, 256), 256)

            @pl.loop(0, mrows // 256)
            def _(m):
                mine = pl.ds(pl.multiple_of(m * 256, 256), 256)
                part = jnp.dot(left[mine, :], right, preferred_element_type=jnp.float32) * scale

                @pl.when(g == 0)
                def _():
                    out_ref[mine, theirs] = part

                @pl.when(g > 0)
                def _():
                    out_ref[mine, theirs] = out_ref[mine, theirs] + part

    def step(t, carry):
        line(pin, up, t - HOP * l, l == 0, l == loops - 1)
        line(sin, down, t - HOP * (loops - 1 - l), l == loops - 1, l == 0)

        done = t - settle

        @pl.when((done >= 0) & (done < count))
        def _():
            at, slot = rows_of(done), slot_of(done)
            total = pin[slot, :] + (sin[slot, :] - own[at, :])
            own[at, :] = total

            @pl.when(far == 0)
            def _():
                cols[core, at, :] = total

        passed = done - REACH * far

        @pl.when((passed >= 0) & (passed < count))
        def _():
            @pl.when(far > 0)
            def _():
                chain(passed).wait_recv()

            @pl.when(far < pairs - 1)
            def _():
                send(chain, passed)

            send(share, passed)

        ready = done - REACH * pairs

        @pl.when((ready >= 0) & (ready < count))
        def _():
            taken(ready).wait_recv()

        @pl.when((ready >= GROUP) & (ready < count + GROUP))
        def _():
            multiply(ready // GROUP - 1, lax.rem(ready, GROUP))

        later = tiles + t // pace

        @pl.when((lax.rem(t, pace) == pace // 2) & (later < tile_count))
        def _():
            half(later)

        return carry

    lax.fori_loop(0, count + HOP * (loops - 1) + REACH * pairs + GROUP, step, 0)

    def drain(i, carry):
        j = count - SLOTS + i

        @pl.when(l < loops - 1)
        def _():
            up(j).wait_send()

        @pl.when(l > 0)
        def _():
            down(j).wait_send()

        @pl.when(far < pairs - 1)
        def _():
            chain(j).wait_send()

        share(j).wait_send()
        return carry

    lax.fori_loop(0, SLOTS, drain, 0)


def local(loops, row_count, integrals, mask, coeffs):
    nslab, naux, mrows, lcols = integrals.shape
    norbit = coeffs.shape[1]
    depth = nslab * naux * norbit
    count = depth // CHUNK
    wide = 2 * TILE
    assert lcols == 2 * mrows and row_count == 2 * loops and norbit % CHUNK == 0
    assert depth % (CHUNK * GROUP) == 0 and 2 * mrows // 256 <= GROUP
    ring = min(count, SLOTS + 3 * HOP * loops)
    spare = (8, 128) if lcols <= depth and norbit <= mrows else (lcols, norbit)
    blocks = jnp.repeat(mask.astype(jnp.float32), TILE, axis=2)
    blocks = blocks.reshape(nslab, mrows // wide, wide // TILE, lcols)
    dma = pltpu.SemaphoreType.DMA
    return pl.pallas_call(
        functools.partial(exchange_kernel, loops, row_count, float(depth) ** -0.5),
        out_shape=jax.ShapeDtypeStruct((mrows, lcols), jnp.float32),
        in_specs=[
            pl.BlockSpec(memory_space=pl.ANY),
            pl.BlockSpec(memory_space=pltpu.VMEM),
            pl.BlockSpec(memory_space=pl.ANY),
        ],
        out_specs=pl.BlockSpec(memory_space=pltpu.VMEM),
        scratch_shapes=[
            pltpu.VMEM((depth, mrows), jnp.float32),
            pltpu.VMEM((ring * CHUNK, mrows), jnp.float32),
            pltpu.VMEM((ring * CHUNK, mrows), jnp.float32),
            pltpu.VMEM((2, depth, mrows), jnp.float32),
            pltpu.VMEM((mrows, 3 * CHUNK * GROUP), jnp.bfloat16),
            pltpu.VMEM((norbit, lcols), jnp.bfloat16),
            pltpu.VMEM((norbit, lcols), jnp.bfloat16),
            pltpu.VMEM((2, wide, lcols), jnp.float32),
            pltpu.VMEM(spare, jnp.float32),
            dma((2,)),
            dma,
        ]
        + [dma((SLOTS,)), dma((count,))] * 4,
        compiler_params=pltpu.CompilerParams(
            collective_id=0, has_side_effects=True, vmem_limit_bytes=67043328
        ),
        name="exchange",
    )(integrals, blocks, coeffs)


def solution(mesh):
    in_specs = (P(None, None, "rows", "loop"), P(None, "rows", "loop"), P("loop", None))
    out_specs = P("rows", "loop")
    body = functools.partial(local, mesh.shape["loop"], mesh.shape["rows"])
    return jax.shard_map(body, mesh=mesh, in_specs=in_specs, out_specs=out_specs, check_vma=False)
```

profile of v0, /device:TPU:4, one launch (start us, length us, event | category | flops | bytes accessed | tf_op | source)
XLA Modules:
  0.0 300.8 jit_solution(15905434814481334301)
XLA Ops:
  0.0 0.7 convert_element_type.3
  0.7 0.1 broadcast_in_dim.3
  0.8 0.7 reshape_reshape.3.mask_ref
  1.5 291.4 %exchange.1 = f32[1024,2048]{1,0:T(8,128)} custom-call(f32[2,2,1024,2048]{3,2,1,0:T(8,128)} %integrals_ref.1, f32[2,4,2,2048]{3,2,1,0:T(2,128)} %reshape_reshape.3.mask_ref, f32[2048,640]{1,0:T(8,128)} %coeffs_ref.1), custom_call_target="tpu_custom_call" | custom-call | tf_op jit(solution)/shard_map/exchange/pallas_call | solution.py:293
  292.9 7.9 %copy.5 = f32[1024,2048]{1,0:T(8,128)} copy(f32[1024,2048]{1,0:T(8,128)} %exchange.1) | data formatting | bytes 16777216
where the time goes:
time: 301 us
  Pallas kernels  291 us (97%)
  local copies, waits for them, and re-layouts  8.71 us (3%)
    pallas_call x1, Pallas kernels, local(): pl.pallas_call(functools.partial(exchange_kernel, loops, row_count, float...  291 us
    unnamed x1, local copies, waits for them, and re-layouts  7.89 us

commit v1 on v0

v1 whole, which is shorter than its diff:
```python
import functools

import jax
import jax.numpy as jnp
from jax import lax
from jax.experimental import pallas as pl
from jax.experimental.pallas import tpu as pltpu
from jax.sharding import PartitionSpec as P

TILE = 128
WIDE = 2 * TILE
CHUNK = 64
SPAN = 256
DEEP = 512
HOP = 3
REACH = 2
SLOTS = 8
BUFFERS = 4
LOAD = 256
MESH = pl.DeviceIdType.MESH


def split(x):
    high = x.astype(jnp.bfloat16)
    low = (x - high.astype(jnp.float32)).astype(jnp.bfloat16)
    return high, low


def ring_place(pair, pairs):
    if pairs == 4:
        return pair + (pair // 2) * (1 - 2 * lax.rem(pair, 2))
    return pair


def place_of(part, tile, block, parts, tiles, norbit):
    inner = tile * norbit + block * TILE
    last = block * (tiles * TILE) + tile * TILE
    if isinstance(part, int):
        return part * tiles * norbit + (inner if part < parts - 1 else last)
    return part * (tiles * norbit) + jnp.where(part < parts - 1, inner, last)


def plan(parts, tiles, norbit, lag, last_done):
    groups, blocks = parts * norbit // SPAN, norbit // TILE
    starts, free = [], 0
    for g in range(groups - 1):
        last = max(
            place_of(h // blocks, tiles - 1, h % blocks, parts, tiles, norbit) + TILE - 1 for h in (2 * g, 2 * g + 1)
        )
        starts.append(max(last // CHUNK + lag, free))
        free = starts[-1] + 1 + 2 * tiles
    return starts + [max(last_done, free)]


def exchange_kernel(
    loops, row_count, integrals_ref, mask_ref, coeffs_ref, acc_ref, left_ref, right_ref,
    own, pin, sin, cols, high_ref, low_ref, tile, room, tile_sem, room_sem,
    up_send, up_recv, dn_send, dn_recv, ch_send, ch_recv, pt_send, pt_recv,
):
    nslab, naux, mrows, lcols = integrals_ref.shape
    norbit = coeffs_ref.shape[1]
    parts = nslab * naux
    tiles = mrows // WIDE
    blocks = norbit // TILE
    tile_count = parts * tiles
    deep = tile.shape[2]
    cuts = lcols // deep
    count = own.shape[0] // CHUNK
    ring = pin.shape[0] // CHUNK
    pairs = row_count // 2
    r, l = lax.axis_index("rows"), lax.axis_index("loop")
    pair, core = r // 2, lax.rem(r, 2)
    partner = r + 1 - 2 * core
    turn = 1 - 2 * core
    place = ring_place(pair, pairs)
    far = lax.rem((place - ring_place(l, pairs)) * turn + pairs, pairs)
    ahead = ring_place(lax.rem(place + turn + pairs, pairs), pairs) * 2 + core
    behind = ring_place(lax.rem(place - turn + pairs, pairs), pairs) * 2 + core

    def deep_of(q):
        return pl.ds(pl.multiple_of(q * deep, deep), deep)

    def row_of(part, m, block):
        return pl.ds(pl.multiple_of(place_of(part, m, block, parts, tiles, norbit), TILE), TILE)

    def fetch(u, q):
        part, m = u // tiles, lax.rem(u, tiles)
        slot = lax.rem(u * cuts + q, BUFFERS)
        return pltpu.make_async_copy(
            integrals_ref.at[
                part // naux, lax.rem(part, naux), pl.ds(pl.multiple_of(m * WIDE, WIDE), WIDE), deep_of(q)
            ],
            tile.at[slot],
            tile_sem.at[slot],
        )

    def fetch_next(u, q):
        i = u * cuts + q + BUFFERS

        @pl.when(i < tile_count * cuts)
        def _():
            fetch(i // cuts, lax.rem(i, cuts)).start()

    def load(n):
        slot = lax.rem(n, 2)
        at = pl.ds(pl.multiple_of(n * LOAD, LOAD), LOAD)
        return pltpu.make_async_copy(coeffs_ref.at[at, :], room.at[slot], room_sem.at[slot])

    def half(u, q):
        part, m = u // tiles, lax.rem(u, tiles)
        slab = part // naux
        fetch(u, q).wait()

        @pl.when(q == 0)
        def _():
            for b in range(blocks):
                own[row_of(part, m, b), :] = jnp.zeros((TILE, WIDE), jnp.float32)

        def piece(i, j):
            keep = mask_ref[slab, m * (WIDE // TILE) + i, q * (deep // TILE) + j].astype(jnp.float32)
            return tile[lax.rem(u * cuts + q, BUFFERS), i * TILE : (i + 1) * TILE, j * TILE : (j + 1) * TILE] * keep

        held = jnp.concatenate(
            [jnp.concatenate([piece(i, j) for j in range(deep // TILE)], axis=1) for i in range(WIDE // TILE)], axis=0
        )
        high, low = split(held)

        def times(a, b):
            return lax.dot_general(a, b, (((1,), (1,)), ((), ())), preferred_element_type=jnp.float32)

        at = deep_of(q)
        value = times(high_ref[:, at], high) + times(high_ref[:, at], low) + times(low_ref[:, at], high)
        for b in range(blocks):
            rows = row_of(part, m, b)
            own[rows, :] = own[rows, :] + value[b * TILE : (b + 1) * TILE]

        fetch_next(u, q)

    for n in range(2):
        load(n).start()
    for i in range(BUFFERS):
        fetch(i // cuts, i % cuts).start()

    barrier = pltpu.get_barrier_semaphore()
    for other in (partner, ahead, behind):
        pl.semaphore_signal(barrier, inc=1, device_id={"rows": other}, device_id_type=MESH)

    @pl.when(l > 0)
    def _():
        pl.semaphore_signal(barrier, inc=1, device_id={"loop": l - 1}, device_id_type=MESH)

    @pl.when(l < loops - 1)
    def _():
        pl.semaphore_signal(barrier, inc=1, device_id={"loop": l + 1}, device_id_type=MESH)

    @pl.loop(0, cuts)
    def _(q):
        for k in range(deep // LOAD):
            n = q * (deep // LOAD) + k
            load(n).wait()
            at = pl.ds(pl.multiple_of(n * LOAD, LOAD), LOAD)
            high_ref[:, at], low_ref[:, at] = split(room[lax.rem(n, 2)].T)

            @pl.when(n + 2 < lcols // LOAD)
            def _():
                load(n + 2).start()

        half(0, q)

    neighbours = jnp.where(l > 0, 1, 0) + jnp.where(l < loops - 1, 1, 0)
    pl.semaphore_wait(barrier, 3 + neighbours)

    def rows_of(j):
        return pl.ds(pl.multiple_of(j * CHUNK, CHUNK), CHUNK)

    def slot_of(j):
        return pl.ds(pl.multiple_of(lax.rem(j, ring) * CHUNK, CHUNK), CHUNK)

    def copy(src, dst, send, recv, j, target):
        return pltpu.make_async_remote_copy(
            src_ref=src, dst_ref=dst, send_sem=send.at[lax.rem(j, SLOTS)], recv_sem=recv.at[j],
            device_id=target, device_id_type=MESH,
        )

    def up(j):
        return copy(pin.at[slot_of(j)], pin.at[slot_of(j)], up_send, up_recv, j, {"loop": l + 1})

    def down(j):
        return copy(sin.at[slot_of(j)], sin.at[slot_of(j)], dn_send, dn_recv, j, {"loop": l - 1})

    def chain(j):
        ref = cols.at[core, rows_of(j)]
        return copy(ref, ref, ch_send, ch_recv, j, {"rows": ahead})

    def share(j):
        ref = cols.at[core, rows_of(j)]
        return copy(ref, ref, pt_send, pt_recv, j, {"rows": partner})

    def taken(j):
        ref = cols.at[1 - core, rows_of(j)]
        return copy(ref, ref, pt_send, pt_recv, j, {"rows": partner})

    def send(make, j):
        @pl.when(j >= SLOTS)
        def _():
            make(j - SLOTS).wait_send()

        make(j).start()

    def line(held, make, j, first, last):
        @pl.when((j >= 0) & (j < count))
        def _():
            at, slot = rows_of(j), slot_of(j)

            @pl.when(first)
            def _():
                held[slot, :] = own[at, :]

            @pl.when(jnp.logical_not(first))
            def _():
                make(j).wait_recv()
                held[slot, :] = held[slot, :] + own[at, :]

            @pl.when(jnp.logical_not(last))
            def _():
                send(make, j)

    settle = HOP * jnp.maximum(l, loops - 1 - l)
    lag = HOP * (loops - 1) + REACH * pairs
    starts = plan(parts, tiles, norbit, lag, count - 1 + HOP * (loops - 1))
    groups = len(starts)
    total_steps = max(count + lag, starts[-1] + 1)
    final = count - 2 * TILE * tiles // CHUNK

    def multiply(g, n):
        @pl.when(n == 0)
        def _():
            @pl.loop(0, tiles)
            def _(m):
                mine = pl.ds(pl.multiple_of(m * WIDE, WIDE), WIDE)
                for h in range(2):
                    block = 2 * g + h
                    high, low = split(own[row_of(block // blocks, m, lax.rem(block, blocks)), :].T)
                    left_ref[mine, h * TILE : (h + 1) * TILE] = high
                    left_ref[mine, SPAN + h * TILE : SPAN + (h + 1) * TILE] = high
                    left_ref[mine, 2 * SPAN + h * TILE : 2 * SPAN + (h + 1) * TILE] = low

        @pl.when(n > 0)
        def _():
            held, m = (n - 1) // tiles, lax.rem(n - 1, tiles)
            both = []
            for h in range(2):
                block = 2 * g + h
                both.append(cols[held, row_of(block // blocks, m, lax.rem(block, blocks)), :])
            high, low = split(jnp.concatenate(both, axis=0))
            right = jnp.concatenate([high, low, high], axis=0)
            theirs = pl.ds(pl.multiple_of((n - 1) * WIDE, WIDE), WIDE)

            @pl.when(g == 0)
            def _():
                acc_ref[:, theirs] = jnp.zeros((mrows, WIDE), jnp.float32)

            acc_ref[:, theirs] = acc_ref[:, theirs] + jnp.dot(left_ref[...], right, preferred_element_type=jnp.float32)

    def step(t, carry):
        line(pin, up, t - HOP * l, l == 0, l == loops - 1)
        line(sin, down, t - HOP * (loops - 1 - l), l == loops - 1, l == 0)

        done = t - settle

        @pl.when((done >= 0) & (done < count))
        def _():
            at, slot = rows_of(done), slot_of(done)
            total = pin[slot, :] + (sin[slot, :] - own[at, :])
            own[at, :] = total

            @pl.when(far == 0)
            def _():
                cols[core, at, :] = total

        passed = done - REACH * far

        @pl.when((passed >= 0) & (passed < count))
        def _():
            @pl.when(far > 0)
            def _():
                chain(passed).wait_recv()

            @pl.when(far < pairs - 1)
            def _():
                send(chain, passed)

            send(share, passed)

        ready = done - REACH * pairs

        @pl.when((ready >= 0) & (ready < count))
        def _():
            taken(ready).wait_recv()

        @pl.when((ready >= final) & (ready < count))
        def _():
            off = (ready - final) * CHUNK
            k = off // (tiles * TILE) * TILE + lax.rem(off, TILE)
            m = lax.rem(off // TILE, tiles)
            for held in range(2):
                high, low = split(cols[held, rows_of(ready), :])
                theirs = pl.ds(pl.multiple_of(held * mrows + m * WIDE, WIDE), WIDE)
                right_ref[pl.ds(pl.multiple_of(k, CHUNK), CHUNK), theirs] = high
                right_ref[pl.ds(pl.multiple_of(SPAN + k, CHUNK), CHUNK), theirs] = low

        g, begin = -1, 0
        for k, at in enumerate(starts):
            g = g + jnp.where(t >= at, 1, 0)
            begin = begin + jnp.where(t >= at, at - (starts[k - 1] if k else 0), 0)

        @pl.when((g >= 0) & (t - begin <= jnp.where(g < groups - 1, 2 * tiles, 0)))
        def _():
            multiply(g, t - begin)

        later, q = 1 + t // (cuts + 1), lax.rem(t, cuts + 1)

        @pl.when((later < tile_count) & (q < cuts))
        def _():
            half(later, q)

        return carry

    lax.fori_loop(0, total_steps, step, 0)

    def drain(i, carry):
        j = count - SLOTS + i

        @pl.when(l < loops - 1)
        def _():
            up(j).wait_send()

        @pl.when(l > 0)
        def _():
            down(j).wait_send()

        @pl.when(far < pairs - 1)
        def _():
            chain(j).wait_send()

        share(j).wait_send()
        return carry

    lax.fori_loop(0, SLOTS, drain, 0)


def finish_kernel(scale, acc_ref, left_ref, right_ref, out_ref):
    right = jnp.concatenate([right_ref[...], right_ref[:SPAN, :]], axis=0)
    value = acc_ref[...] + jnp.dot(left_ref[...], right, preferred_element_type=jnp.float32)
    out_ref[...] = value * scale


def local(loops, row_count, integrals, mask, coeffs):
    nslab, naux, mrows, lcols = integrals.shape
    norbit = coeffs.shape[1]
    depth = nslab * naux * norbit
    tiles = mrows // WIDE
    count = depth * tiles * WIDE // (CHUNK * WIDE)
    assert lcols == 2 * mrows and row_count == 2 * loops and mrows % WIDE == 0
    assert norbit % TILE == 0 and norbit >= SPAN and depth % SPAN == 0
    deep = min(DEEP, lcols)
    cuts = lcols // deep
    assert cuts + 1 <= norbit // CHUNK and nslab * naux * tiles * cuts >= BUFFERS and lcols >= 2 * LOAD
    ring = min(count, max(SLOTS + 2 * HOP, HOP * (loops + 1)) + 4)
    dma = pltpu.SemaphoreType.DMA
    vmem = pl.BlockSpec(memory_space=pltpu.VMEM)
    partial = pl.pallas_call(
        functools.partial(exchange_kernel, loops, row_count),
        out_shape=[
            jax.ShapeDtypeStruct((mrows, lcols), jnp.float32),
            jax.ShapeDtypeStruct((mrows, 3 * SPAN), jnp.bfloat16),
            jax.ShapeDtypeStruct((2 * SPAN, lcols), jnp.bfloat16),
        ],
        in_specs=[
            pl.BlockSpec(memory_space=pltpu.MemorySpace.HBM),
            pl.BlockSpec(memory_space=pltpu.SMEM),
            pl.BlockSpec(memory_space=pltpu.MemorySpace.HBM),
        ],
        out_specs=[vmem] * 3,
        scratch_shapes=[
            pltpu.VMEM((depth * tiles, WIDE), jnp.float32),
            pltpu.VMEM((ring * CHUNK, WIDE), jnp.float32),
            pltpu.VMEM((ring * CHUNK, WIDE), jnp.float32),
            pltpu.VMEM((2, depth * tiles, WIDE), jnp.float32),
            pltpu.VMEM((norbit, lcols), jnp.bfloat16),
            pltpu.VMEM((norbit, lcols), jnp.bfloat16),
            pltpu.VMEM((BUFFERS, WIDE, deep), jnp.float32),
            pltpu.VMEM((2, LOAD, norbit), jnp.float32),
            dma((BUFFERS,)),
            dma((2,)),
        ]
        + [dma((SLOTS,)), dma((count,))] * 4,
        compiler_params=pltpu.CompilerParams(
            collective_id=0, has_side_effects=True, vmem_limit_bytes=42 << 20
        ),
        name="exchange",
    )(integrals, mask, pltpu.with_memory_space_constraint(coeffs, pltpu.MemorySpace.HBM))
    return pl.pallas_call(
        functools.partial(finish_kernel, float(depth) ** -0.5),
        grid=(lcols // WIDE,),
        out_shape=jax.ShapeDtypeStruct((mrows, lcols), jnp.float32),
        in_specs=[
            pl.BlockSpec((mrows, WIDE), lambda n: (0, n)),
            pl.BlockSpec((mrows, 3 * SPAN), lambda n: (0, 0)),
            pl.BlockSpec((2 * SPAN, WIDE), lambda n: (0, n)),
        ],
        out_specs=pl.BlockSpec((mrows, WIDE), lambda n: (0, n)),
        compiler_params=pltpu.CompilerParams(vmem_limit_bytes=14 << 20),
        name="finish",
    )(*partial)


def solution(mesh):
    in_specs = (P(None, None, "rows", "loop"), P(None, "rows", "loop"), P("loop", None))
    out_specs = P("rows", "loop")
    body = functools.partial(local, mesh.shape["loop"], mesh.shape["rows"])
    return jax.shard_map(body, mesh=mesh, in_specs=in_specs, out_specs=out_specs, check_vma=False)
```

time: 301 us -> 275 us (0.914)
  Pallas kernels: 291 us -> 273 us
  local copies, waits for them, and re-layouts: 8.71 us -> 0.7 us
    pallas_call x1 -> x2, Pallas kernels: 291 us -> 273 us  [the longest x1 266 us: local(): pl.pallas_call(functools.partial(exchange_kernel, loops, row_count), out_...]
    unnamed x1 -> x2, local copies, waits for them, and re-layouts: 7.89 us -> 0.7 us
where the time goes in v1:
time: 275 us; the launch traced here: 274 us
  Pallas kernels  273 us (99%)
    pallas_call x1, Pallas kernels, local(): pl.pallas_call(functools.partial(exchange_kernel, loops, row_count), out_...  266 us
    pallas_call x1, Pallas kernels, local(): pl.pallas_call(functools.partial(finish_kernel, float(depth) ** (-0.5)),...  7.61 us

profile of v1, /device:TPU:4, one launch (start us, length us, event | category | flops | bytes accessed | tf_op | source)
XLA Modules:
  0.0 273.9 jit_solution(16825285552008076623)
XLA Ops:
  0.0 0.0 copy-start
  0.0 0.7 copy-done
  0.7 265.6 %exchange.1 = (f32[1024,2048]{1,0:T(8,128)S(1)}, bf16[1024,768]{1,0:T(8,128)(2,1)S(1)}, bf16[512,2048]{1,0:T(8,128)(2,1)S(1)}) custom-call(f32[2,2,1024,2048]{3,2,1,0:T(8,128)} %integrals_ref.1, s32[2,8,16]{2,1,0:T(8,128)S(1)} %copy-done, f32[2048,640]{1,0:T(8,128)} %coeffs_ref.1), custom_call_target="tpu_custom_call" | custom-call | tf_op jit(solution)/shard_map/exchange/pallas_call | solution.py:372
  266.3 7.6 %finish.1 = f32[1024,2048]{1,0:T(8,128)} custom-call(f32[1024,2048]{1,0:T(8,128)S(1)} %get-tuple-element.8.acc_ref, bf16[1024,768]{1,0:T(8,128)(2,1)S(1)} %get-tuple-element.9.left_ref, bf16[512,2048]{1,0:T(8,128)(2,1)S(1)} %get-tuple-element.10.right_ref), custom_call_target="tpu_custom_call" | custom-call | tf_op jit(solution)/shard_map/finish/pallas_call | solution.py:403
Async XLA Ops:
  0.0 0.7 copy-start

commit v2 on v1

--- a/solution.py
+++ b/solution.py
@@ -12,11 +12,11 @@
 CHUNK = 64
 SPAN = 256
 DEEP = 512
-HOP = 3
-REACH = 2
+HOP = 4
+REACH = 3
 SLOTS = 8
-BUFFERS = 4
-LOAD = 256
+BUFFERS = 6
+BROAD = 512
 MESH = pl.DeviceIdType.MESH
 
 
@@ -54,7 +54,7 @@
 
 def exchange_kernel(
     loops, row_count, integrals_ref, mask_ref, coeffs_ref, acc_ref, left_ref, right_ref,
-    own, pin, sin, cols, high_ref, low_ref, tile, room, tile_sem, room_sem,
+    own, pin, sin, cols, high_ref, low_ref, tile, spare, tile_sem, load_sem,
     up_send, up_recv, dn_send, dn_recv, ch_send, ch_recv, pt_send, pt_recv,
 ):
     nslab, naux, mrows, lcols = integrals_ref.shape
@@ -65,6 +65,7 @@
     tile_count = parts * tiles
     deep = tile.shape[2]
     cuts = lcols // deep
+    buffers = tile.shape[0]
     count = own.shape[0] // CHUNK
     ring = pin.shape[0] // CHUNK
     pairs = row_count // 2
@@ -85,7 +86,7 @@
 
     def fetch(u, q):
         part, m = u // tiles, lax.rem(u, tiles)
-        slot = lax.rem(u * cuts + q, BUFFERS)
+        slot = lax.rem(u * cuts + q, buffers)
         return pltpu.make_async_copy(
             integrals_ref.at[
                 part // naux, lax.rem(part, naux), pl.ds(pl.multiple_of(m * WIDE, WIDE), WIDE), deep_of(q)
@@ -95,30 +96,50 @@
         )
 
     def fetch_next(u, q):
-        i = u * cuts + q + BUFFERS
+        i = u * cuts + q + buffers
 
         @pl.when(i < tile_count * cuts)
         def _():
             fetch(i // cuts, lax.rem(i, cuts)).start()
 
-    def load(n):
-        slot = lax.rem(n, 2)
-        at = pl.ds(pl.multiple_of(n * LOAD, LOAD), LOAD)
-        return pltpu.make_async_copy(coeffs_ref.at[at, :], room.at[slot], room_sem.at[slot])
-
-    def half(u, q):
+    ranges = ((0, SPAN), (SPAN, norbit))
+
+    def landing(q, k):
+        low, high = ranges[k]
+        if spare.shape == coeffs_ref.shape:
+            return spare.at[deep_of(q), low:high]
+        first, rows = q * deep // mrows, lax.rem(q * deep, mrows)
+        at = pl.ds(pl.multiple_of(first * norbit + low, TILE), high - low)
+        return acc_ref.at[pl.ds(pl.multiple_of(rows, deep), deep), at]
+
+    def load(q, k):
+        return pltpu.make_async_copy(
+            coeffs_ref.at[deep_of(q), ranges[k][0] : ranges[k][1]], landing(q, k), load_sem.at[k, q]
+        )
+
+    def prepare(q, k):
+        load(q, k).wait()
+        rows = slice(*ranges[k])
+        held = landing(q, k)
+        for n in range(deep // 256):
+            at = pl.ds(pl.multiple_of(q * deep + n * 256, 256), 256)
+            high_ref[rows, at], low_ref[rows, at] = split(held[n * 256 : (n + 1) * 256, :].T)
+
+    def half(u, q, first, last):
         part, m = u // tiles, lax.rem(u, tiles)
         slab = part // naux
-        fetch(u, q).wait()
+        own_blocks = range(first // TILE, last // TILE)
+        if first == 0:
+            fetch(u, q).wait()
 
         @pl.when(q == 0)
         def _():
-            for b in range(blocks):
+            for b in own_blocks:
                 own[row_of(part, m, b), :] = jnp.zeros((TILE, WIDE), jnp.float32)
 
         def piece(i, j):
             keep = mask_ref[slab, m * (WIDE // TILE) + i, q * (deep // TILE) + j].astype(jnp.float32)
-            return tile[lax.rem(u * cuts + q, BUFFERS), i * TILE : (i + 1) * TILE, j * TILE : (j + 1) * TILE] * keep
+            return tile[lax.rem(u * cuts + q, buffers), i * TILE : (i + 1) * TILE, j * TILE : (j + 1) * TILE] * keep
 
         held = jnp.concatenate(
             [jnp.concatenate([piece(i, j) for j in range(deep // TILE)], axis=1) for i in range(WIDE // TILE)], axis=0
@@ -129,16 +150,21 @@
             return lax.dot_general(a, b, (((1,), (1,)), ((), ())), preferred_element_type=jnp.float32)
 
         at = deep_of(q)
-        value = times(high_ref[:, at], high) + times(high_ref[:, at], low) + times(low_ref[:, at], high)
-        for b in range(blocks):
+        upper, lower = high_ref[first:last, at], low_ref[first:last, at]
+        value = times(upper, high) + times(upper, low) + times(lower, high)
+        for b in own_blocks:
             rows = row_of(part, m, b)
-            own[rows, :] = own[rows, :] + value[b * TILE : (b + 1) * TILE]
-
-        fetch_next(u, q)
-
-    for n in range(2):
-        load(n).start()
-    for i in range(BUFFERS):
+            own[rows, :] = own[rows, :] + value[b * TILE - first : (b + 1) * TILE - first]
+
+        if last == norbit:
+            fetch_next(u, q)
+
+    for q in range(cuts):
+        load(q, 0).start()
+        fetch(0, q).start()
+    for q in range(cuts):
+        load(q, 1).start()
+    for i in range(cuts, buffers):
         fetch(i // cuts, i % cuts).start()
 
     barrier = pltpu.get_barrier_semaphore()
@@ -155,17 +181,8 @@
 
     @pl.loop(0, cuts)
     def _(q):
-        for k in range(deep // LOAD):
-            n = q * (deep // LOAD) + k
-            load(n).wait()
-            at = pl.ds(pl.multiple_of(n * LOAD, LOAD), LOAD)
-            high_ref[:, at], low_ref[:, at] = split(room[lax.rem(n, 2)].T)
-
-            @pl.when(n + 2 < lcols // LOAD)
-            def _():
-                load(n + 2).start()
-
-        half(0, q)
+        prepare(q, 0)
+        half(0, q, 0, SPAN)
 
     neighbours = jnp.where(l > 0, 1, 0) + jnp.where(l < loops - 1, 1, 0)
     pl.semaphore_wait(barrier, 3 + neighbours)
@@ -318,11 +335,16 @@
         def _():
             multiply(g, t - begin)
 
-        later, q = 1 + t // (cuts + 1), lax.rem(t, cuts + 1)
-
-        @pl.when((later < tile_count) & (q < cuts))
-        def _():
-            half(later, q)
+        @pl.when(t < cuts)
+        def _():
+            prepare(t, 1)
+            half(0, t, SPAN, norbit)
+
+        later, q = 1 + (t - cuts) // (cuts + 1), lax.rem(t - cuts, cuts + 1)
+
+        @pl.when((t >= cuts) & (later < tile_count) & (q < cuts))
+        def _():
+            half(later, q, 0, norbit)
 
         return carry
 
@@ -350,8 +372,10 @@
 
 
 def finish_kernel(scale, acc_ref, left_ref, right_ref, out_ref):
-    right = jnp.concatenate([right_ref[...], right_ref[:SPAN, :]], axis=0)
-    value = acc_ref[...] + jnp.dot(left_ref[...], right, preferred_element_type=jnp.float32)
+    broad = out_ref.shape[1]
+    at = pl.ds(pl.multiple_of(pl.program_id(0) * broad, broad), broad)
+    right = jnp.concatenate([right_ref[:, at], right_ref[:SPAN, at]], axis=0)
+    value = acc_ref[:, at] + jnp.dot(left_ref[...], right, preferred_element_type=jnp.float32)
     out_ref[...] = value * scale
 
 
@@ -365,10 +389,14 @@
     assert norbit % TILE == 0 and norbit >= SPAN and depth % SPAN == 0
     deep = min(DEEP, lcols)
     cuts = lcols // deep
-    assert cuts + 1 <= norbit // CHUNK and nslab * naux * tiles * cuts >= BUFFERS and lcols >= 2 * LOAD
-    ring = min(count, max(SLOTS + 2 * HOP, HOP * (loops + 1)) + 4)
+    buffers = min(BUFFERS, nslab * naux * tiles * cuts)
+    assert cuts + 1 <= norbit // CHUNK and cuts <= min(buffers, SPAN // CHUNK) and norbit > SPAN
+    spare = (8, 128) if 2 * norbit <= lcols and mrows % deep == 0 else (lcols, norbit)
+    broad = min(BROAD, lcols)
+    ring = min(count, max(SLOTS + 2 * HOP, HOP * (loops - 1)) + 2)
     dma = pltpu.SemaphoreType.DMA
     vmem = pl.BlockSpec(memory_space=pltpu.VMEM)
+    held = functools.partial(pltpu.with_memory_space_constraint, memory_space=pltpu.MemorySpace.HBM)
     partial = pl.pallas_call(
         functools.partial(exchange_kernel, loops, row_count),
         out_shape=[
@@ -377,9 +405,9 @@
             jax.ShapeDtypeStruct((2 * SPAN, lcols), jnp.bfloat16),
         ],
         in_specs=[
-            pl.BlockSpec(memory_space=pltpu.MemorySpace.HBM),
+            pl.BlockSpec(memory_space=pl.ANY),
             pl.BlockSpec(memory_space=pltpu.SMEM),
-            pl.BlockSpec(memory_space=pltpu.MemorySpace.HBM),
+            pl.BlockSpec(memory_space=pl.ANY),
         ],
         out_specs=[vmem] * 3,
         scratch_shapes=[
@@ -389,27 +417,23 @@
             pltpu.VMEM((2, depth * tiles, WIDE), jnp.float32),
             pltpu.VMEM((norbit, lcols), jnp.bfloat16),
             pltpu.VMEM((norbit, lcols), jnp.bfloat16),
-            pltpu.VMEM((BUFFERS, WIDE, deep), jnp.float32),
-            pltpu.VMEM((2, LOAD, norbit), jnp.float32),
-            dma((BUFFERS,)),
-            dma((2,)),
+            pltpu.VMEM((buffers, WIDE, deep), jnp.float32),
+            pltpu.VMEM(spare, jnp.float32),
+            dma((buffers,)),
+            dma((2, cuts)),
         ]
         + [dma((SLOTS,)), dma((count,))] * 4,
         compiler_params=pltpu.CompilerParams(
             collective_id=0, has_side_effects=True, vmem_limit_bytes=42 << 20
         ),
         name="exchange",
-    )(integrals, mask, pltpu.with_memory_space_constraint(coeffs, pltpu.MemorySpace.HBM))
+    )(integrals, held(mask), held(coeffs))
     return pl.pallas_call(
         functools.partial(finish_kernel, float(depth) ** -0.5),
-        grid=(lcols // WIDE,),
+        grid=(lcols // broad,),
         out_shape=jax.ShapeDtypeStruct((mrows, lcols), jnp.float32),
-        in_specs=[
-            pl.BlockSpec((mrows, WIDE), lambda n: (0, n)),
-            pl.BlockSpec((mrows, 3 * SPAN), lambda n: (0, 0)),
-            pl.BlockSpec((2 * SPAN, WIDE), lambda n: (0, n)),
-        ],
-        out_specs=pl.BlockSpec((mrows, WIDE), lambda n: (0, n)),
+        in_specs=[vmem] * 3,
+        out_specs=pl.BlockSpec((mrows, broad), lambda n: (0, n)),
         compiler_params=pltpu.CompilerParams(vmem_limit_bytes=14 << 20),
         name="finish",
     )(*partial)

time: 275 us -> 266 us (0.967)
  Pallas kernels: 273 us -> 264 us
    pallas_call x1, Pallas kernels: 266 us -> 258 us  [local(): pl.pallas_call(functools.partial(exchange_kernel, loops, row_count), out_...]
where the time goes in v2:
time: 266 us; the launch traced here: 264 us
  Pallas kernels  264 us (99%)
    pallas_call x1, Pallas kernels, local(): pl.pallas_call(functools.partial(exchange_kernel, loops, row_count), out_...  258 us
    pallas_call x1, Pallas kernels, local(): pl.pallas_call(functools.partial(finish_kernel, float(depth) ** (-0.5)),...  5.61 us

profile of v2, /device:TPU:4, one launch (start us, length us, event | category | flops | bytes accessed | tf_op | source)
XLA Modules:
  0.0 263.8 jit_solution(11033692762466187048)
XLA Ops:
  0.0 258.1 %exchange.1 = (f32[1024,2048]{1,0:T(8,128)S(1)}, bf16[1024,768]{1,0:T(8,128)(2,1)S(1)}, bf16[512,2048]{1,0:T(8,128)(2,1)S(1)}) custom-call(f32[2,2,1024,2048]{3,2,1,0:T(8,128)} %integrals_ref.1, s32[2,8,16]{2,1,0:T(8,128)} %mask_ref.1, f32[2048,640]{1,0:T(8,128)} %coeffs_ref.1), custom_call_target="tpu_custom_call" | custom-call | tf_op jit(solution)/shard_map/exchange/pallas_call | solution.py:400
  258.2 5.6 %finish.1 = f32[1024,2048]{1,0:T(8,128)} custom-call(f32[1024,2048]{1,0:T(8,128)S(1)} %get-tuple-element.8.acc_ref, bf16[1024,768]{1,0:T(8,128)(2,1)S(1)} %get-tuple-element.9.left_ref, bf16[512,2048]{1,0:T(8,128)(2,1)S(1)} %get-tuple-element.10.right_ref), custom_call_target="tpu_custom_call" | custom-call | tf_op jit(solution)/shard_map/finish/pallas_call | solution.py:431

commit v3 on v2

--- a/solution.py
+++ b/solution.py
@@ -12,7 +12,7 @@
 CHUNK = 64
 SPAN = 256
 DEEP = 512
-HOP = 4
+HOP = 3
 REACH = 3
 SLOTS = 8
 BUFFERS = 6
@@ -55,7 +55,7 @@
 def exchange_kernel(
     loops, row_count, integrals_ref, mask_ref, coeffs_ref, acc_ref, left_ref, right_ref,
     own, pin, sin, cols, high_ref, low_ref, tile, spare, tile_sem, load_sem,
-    up_send, up_recv, dn_send, dn_recv, ch_send, ch_recv, pt_send, pt_recv,
+    keep_ref, keep_sem, up_send, up_recv, dn_send, dn_recv, ch_send, ch_recv, pt_send, pt_recv, bk_send,
 ):
     nslab, naux, mrows, lcols = integrals_ref.shape
     norbit = coeffs_ref.shape[1]
@@ -77,6 +77,10 @@
     far = lax.rem((place - ring_place(l, pairs)) * turn + pairs, pairs)
     ahead = ring_place(lax.rem(place + turn + pairs, pairs), pairs) * 2 + core
     behind = ring_place(lax.rem(place - turn + pairs, pairs), pairs) * 2 + core
+    longest = pairs // 2
+    hops = jnp.where(far <= longest, far, pairs - far)
+    forward = far < longest
+    backward = ((far == 0) & (longest < pairs - 1)) | (far > longest + 1)
 
     def deep_of(q):
         return pl.ds(pl.multiple_of(q * deep, deep), deep)
@@ -138,7 +142,7 @@
                 own[row_of(part, m, b), :] = jnp.zeros((TILE, WIDE), jnp.float32)
 
         def piece(i, j):
-            keep = mask_ref[slab, m * (WIDE // TILE) + i, q * (deep // TILE) + j].astype(jnp.float32)
+            keep = keep_ref[slab, m * (WIDE // TILE) + i, q * (deep // TILE) + j].astype(jnp.float32)
             return tile[lax.rem(u * cuts + q, buffers), i * TILE : (i + 1) * TILE, j * TILE : (j + 1) * TILE] * keep
 
         held = jnp.concatenate(
@@ -159,6 +163,8 @@
         if last == norbit:
             fetch_next(u, q)
 
+    taken_mask = pltpu.make_async_copy(mask_ref, keep_ref, keep_sem)
+    taken_mask.start()
     for q in range(cuts):
         load(q, 0).start()
         fetch(0, q).start()
@@ -179,6 +185,8 @@
     def _():
         pl.semaphore_signal(barrier, inc=1, device_id={"loop": l + 1}, device_id_type=MESH)
 
+    taken_mask.wait()
+
     @pl.loop(0, cuts)
     def _(q):
         prepare(q, 0)
@@ -209,6 +217,10 @@
         ref = cols.at[core, rows_of(j)]
         return copy(ref, ref, ch_send, ch_recv, j, {"rows": ahead})
 
+    def back(j):
+        ref = cols.at[core, rows_of(j)]
+        return copy(ref, ref, bk_send, ch_recv, j, {"rows": behind})
+
     def share(j):
         ref = cols.at[core, rows_of(j)]
         return copy(ref, ref, pt_send, pt_recv, j, {"rows": partner})
@@ -243,7 +255,7 @@
                 send(make, j)
 
     settle = HOP * jnp.maximum(l, loops - 1 - l)
-    lag = HOP * (loops - 1) + REACH * pairs
+    lag = HOP * (loops - 1) + REACH * (longest + 1)
     starts = plan(parts, tiles, norbit, lag, count - 1 + HOP * (loops - 1))
     groups = len(starts)
     total_steps = max(count + lag, starts[-1] + 1)
@@ -295,7 +307,7 @@
             def _():
                 cols[core, at, :] = total
 
-        passed = done - REACH * far
+        passed = done - REACH * hops
 
         @pl.when((passed >= 0) & (passed < count))
         def _():
@@ -303,13 +315,17 @@
             def _():
                 chain(passed).wait_recv()
 
-            @pl.when(far < pairs - 1)
+            @pl.when(forward)
             def _():
                 send(chain, passed)
 
+            @pl.when(backward)
+            def _():
+                send(back, passed)
+
             send(share, passed)
 
-        ready = done - REACH * pairs
+        ready = done - REACH * (longest + 1)
 
         @pl.when((ready >= 0) & (ready < count))
         def _():
@@ -361,9 +377,13 @@
         def _():
             down(j).wait_send()
 
-        @pl.when(far < pairs - 1)
+        @pl.when(forward)
         def _():
             chain(j).wait_send()
+
+        @pl.when(backward)
+        def _():
+            back(j).wait_send()
 
         share(j).wait_send()
         return carry
@@ -406,7 +426,7 @@
         ],
         in_specs=[
             pl.BlockSpec(memory_space=pl.ANY),
-            pl.BlockSpec(memory_space=pltpu.SMEM),
+            pl.BlockSpec(memory_space=pl.ANY),
             pl.BlockSpec(memory_space=pl.ANY),
         ],
         out_specs=[vmem] * 3,
@@ -422,7 +442,9 @@
             dma((buffers,)),
             dma((2, cuts)),
         ]
-        + [dma((SLOTS,)), dma((count,))] * 4,
+        + [pltpu.SMEM(mask.shape, mask.dtype), dma]
+        + [dma((SLOTS,)), dma((count,))] * 4
+        + [dma((SLOTS,))],
         compiler_params=pltpu.CompilerParams(
             collective_id=0, has_side_effects=True, vmem_limit_bytes=42 << 20
         ),

time: 266 us -> 262 us (0.985); the launches traced: 264 us -> 257 us
  Pallas kernels: 264 us -> 257 us
    pallas_call x1, Pallas kernels: 258 us -> 251 us  [local(): pl.pallas_call(functools.partial(exchange_kernel, loops, row_count), out_...]
where the time goes in v3:
time: 262 us; the launch traced here: 257 us
  Pallas kernels  257 us (98%)
    pallas_call x1, Pallas kernels, local(): pl.pallas_call(functools.partial(exchange_kernel, loops, row_count), out_...  251 us
    pallas_call x1, Pallas kernels, local(): pl.pallas_call(functools.partial(finish_kernel, float(depth) ** (-0.5)),...  5.62 us

profile of v3, /device:TPU:4, one launch (start us, length us, event | category | flops | bytes accessed | tf_op | source)
XLA Modules:
  0.0 257.1 jit_solution(60765359526147829)
XLA Ops:
  0.0 251.5 %exchange.1 = (f32[1024,2048]{1,0:T(8,128)S(1)}, bf16[1024,768]{1,0:T(8,128)(2,1)S(1)}, bf16[512,2048]{1,0:T(8,128)(2,1)S(1)}) custom-call(f32[2,2,1024,2048]{3,2,1,0:T(8,128)} %integrals_ref.1, s32[2,8,16]{2,1,0:T(8,128)} %mask_ref.1, f32[2048,640]{1,0:T(8,128)} %coeffs_ref.1), custom_call_target="tpu_custom_call" | custom-call | tf_op jit(solution)/shard_map/exchange/pallas_call | solution.py:420
  251.5 5.6 %finish.1 = f32[1024,2048]{1,0:T(8,128)} custom-call(f32[1024,2048]{1,0:T(8,128)S(1)} %get-tuple-element.8.acc_ref, bf16[1024,768]{1,0:T(8,128)(2,1)S(1)} %get-tuple-element.9.left_ref, bf16[512,2048]{1,0:T(8,128)(2,1)S(1)} %get-tuple-element.10.right_ref), custom_call_target="tpu_custom_call" | custom-call | tf_op jit(solution)/shard_map/finish/pallas_call | solution.py:453

commit v4 on v3

--- a/solution.py
+++ b/solution.py
@@ -40,9 +40,9 @@
     return part * (tiles * norbit) + jnp.where(part < parts - 1, inner, last)
 
 
-def plan(parts, tiles, norbit, lag, last_done):
+def plan(parts, tiles, norbit, lag, last_done, free):
     groups, blocks = parts * norbit // SPAN, norbit // TILE
-    starts, free = [], 0
+    starts = []
     for g in range(groups - 1):
         last = max(
             place_of(h // blocks, tiles - 1, h % blocks, parts, tiles, norbit) + TILE - 1 for h in (2 * g, 2 * g + 1)
@@ -203,7 +203,7 @@
 
     def copy(src, dst, send, recv, j, target):
         return pltpu.make_async_remote_copy(
-            src_ref=src, dst_ref=dst, send_sem=send.at[lax.rem(j, SLOTS)], recv_sem=recv.at[j],
+            src_ref=src, dst_ref=dst, send_sem=send.at[lax.rem(j, SLOTS)], recv_sem=recv.at[lax.rem(j, recv.shape[0])],
             device_id=target, device_id_type=MESH,
         )
 
@@ -256,7 +256,7 @@
 
     settle = HOP * jnp.maximum(l, loops - 1 - l)
     lag = HOP * (loops - 1) + REACH * (longest + 1)
-    starts = plan(parts, tiles, norbit, lag, count - 1 + HOP * (loops - 1))
+    starts = plan(parts, tiles, norbit, lag, count - 1 + HOP * (loops - 1), cuts + (tile_count - 1) * (cuts + 1))
     groups = len(starts)
     total_steps = max(count + lag, starts[-1] + 1)
     final = count - 2 * TILE * tiles // CHUNK
@@ -414,6 +414,7 @@
     spare = (8, 128) if 2 * norbit <= lcols and mrows % deep == 0 else (lcols, norbit)
     broad = min(BROAD, lcols)
     ring = min(count, max(SLOTS + 2 * HOP, HOP * (loops - 1)) + 2)
+    lag, line = HOP * (loops - 1) + REACH * (row_count // 4 + 1), 2 * HOP + 6
     dma = pltpu.SemaphoreType.DMA
     vmem = pl.BlockSpec(memory_space=pltpu.VMEM)
     held = functools.partial(pltpu.with_memory_space_constraint, memory_space=pltpu.MemorySpace.HBM)
@@ -443,8 +444,7 @@
             dma((2, cuts)),
         ]
         + [pltpu.SMEM(mask.shape, mask.dtype), dma]
-        + [dma((SLOTS,)), dma((count,))] * 4
-        + [dma((SLOTS,))],
+        + [dma((min(count, slots),)) for slots in (SLOTS, line, SLOTS, line, SLOTS, 2 * lag + 4, SLOTS, lag + 10, SLOTS)],
         compiler_params=pltpu.CompilerParams(
             collective_id=0, has_side_effects=True, vmem_limit_bytes=42 << 20
         ),

time: 262 us -> 254 us (0.969)
  Pallas kernels: 257 us -> 250 us
    pallas_call x1, Pallas kernels: 251 us -> 244 us  [local(): pl.pallas_call(functools.partial(exchange_kernel, loops, row_count), out_...]
where the time goes in v4:
time: 254 us; the launch traced here: 250 us
  Pallas kernels  250 us (98%)
    pallas_call x1, Pallas kernels, local(): pl.pallas_call(functools.partial(exchange_kernel, loops, row_count), out_...  244 us
    pallas_call x1, Pallas kernels, local(): pl.pallas_call(functools.partial(finish_kernel, float(depth) ** (-0.5)),...  5.61 us

profile of v4, /device:TPU:4, one launch (start us, length us, event | category | flops | bytes accessed | tf_op | source)
XLA Modules:
  0.0 249.8 jit_solution(12785151645314309613)
XLA Ops:
  0.0 244.1 %exchange.1 = (f32[1024,2048]{1,0:T(8,128)S(1)}, bf16[1024,768]{1,0:T(8,128)(2,1)S(1)}, bf16[512,2048]{1,0:T(8,128)(2,1)S(1)}) custom-call(f32[2,2,1024,2048]{3,2,1,0:T(8,128)} %integrals_ref.1, s32[2,8,16]{2,1,0:T(8,128)} %mask_ref.1, f32[2048,640]{1,0:T(8,128)} %coeffs_ref.1), custom_call_target="tpu_custom_call" | custom-call | tf_op jit(solution)/shard_map/exchange/pallas_call | solution.py:421
  244.2 5.6 %finish.1 = f32[1024,2048]{1,0:T(8,128)} custom-call(f32[1024,2048]{1,0:T(8,128)S(1)} %get-tuple-element.8.acc_ref, bf16[1024,768]{1,0:T(8,128)(2,1)S(1)} %get-tuple-element.9.left_ref, bf16[512,2048]{1,0:T(8,128)(2,1)S(1)} %get-tuple-element.10.right_ref), custom_call_target="tpu_custom_call" | custom-call | tf_op jit(solution)/shard_map/finish/pallas_call | solution.py:453

commit v5 on v4

--- a/solution.py
+++ b/solution.py
@@ -14,7 +14,7 @@
 DEEP = 512
 HOP = 3
 REACH = 3
-SLOTS = 8
+SLOTS = 4
 BUFFERS = 6
 BROAD = 512
 MESH = pl.DeviceIdType.MESH
@@ -256,7 +256,8 @@
 
     settle = HOP * jnp.maximum(l, loops - 1 - l)
     lag = HOP * (loops - 1) + REACH * (longest + 1)
-    starts = plan(parts, tiles, norbit, lag, count - 1 + HOP * (loops - 1), cuts + (tile_count - 1) * (cuts + 1))
+    halves = cuts + (tile_count - 1) * (cuts + 1) + HOP * ((loops - 1) // 2)
+    starts = plan(parts, tiles, norbit, lag, count - 1 + HOP * (loops - 1), halves)
     groups = len(starts)
     total_steps = max(count + lag, starts[-1] + 1)
     final = count - 2 * TILE * tiles // CHUNK
@@ -351,14 +352,17 @@
         def _():
             multiply(g, t - begin)
 
-        @pl.when(t < cuts)
-        def _():
-            prepare(t, 1)
-            half(0, t, SPAN, norbit)
-
-        later, q = 1 + (t - cuts) // (cuts + 1), lax.rem(t - cuts, cuts + 1)
-
-        @pl.when((t >= cuts) & (later < tile_count) & (q < cuts))
+        since = t - HOP * jnp.minimum(l, loops - 1 - l)
+
+        @pl.when((since >= 0) & (since < cuts))
+        def _():
+            prepare(since, 1)
+            half(0, since, SPAN, norbit)
+
+        past = since - cuts
+        later, q = 1 + past // (cuts + 1), lax.rem(past, cuts + 1)
+
+        @pl.when((past >= 0) & (later < tile_count) & (q < cuts))
         def _():
             half(later, q, 0, norbit)
 
@@ -413,8 +417,8 @@
     assert cuts + 1 <= norbit // CHUNK and cuts <= min(buffers, SPAN // CHUNK) and norbit > SPAN
     spare = (8, 128) if 2 * norbit <= lcols and mrows % deep == 0 else (lcols, norbit)
     broad = min(BROAD, lcols)
-    ring = min(count, max(SLOTS + 2 * HOP, HOP * (loops - 1)) + 2)
-    lag, line = HOP * (loops - 1) + REACH * (row_count // 4 + 1), 2 * HOP + 6
+    ring = min(count, max(SLOTS + 2 * HOP, HOP * (loops - 1)) + 6)
+    lag, line = HOP * (loops - 1) + REACH * (row_count // 4 + 1), HOP * loops
     dma = pltpu.SemaphoreType.DMA
     vmem = pl.BlockSpec(memory_space=pltpu.VMEM)
     held = functools.partial(pltpu.with_memory_space_constraint, memory_space=pltpu.MemorySpace.HBM)
@@ -444,7 +448,7 @@
             dma((2, cuts)),
         ]
         + [pltpu.SMEM(mask.shape, mask.dtype), dma]
-        + [dma((min(count, slots),)) for slots in (SLOTS, line, SLOTS, line, SLOTS, 2 * lag + 4, SLOTS, lag + 10, SLOTS)],
+        + [dma((min(count, slots),)) for slots in (SLOTS, line, SLOTS, line, SLOTS, 2 * lag, SLOTS, lag + 8, SLOTS)],
         compiler_params=pltpu.CompilerParams(
             collective_id=0, has_side_effects=True, vmem_limit_bytes=42 << 20
         ),

time: 254 us -> 254 us (level)
  no operation moved by 1% of the time
where the time goes in v5:
time: 254 us; the launch traced here: 250 us
  Pallas kernels  249 us (98%)
    pallas_call x1, Pallas kernels, local(): pl.pallas_call(functools.partial(exchange_kernel, loops, row_count), out_...  244 us
    pallas_call x1, Pallas kernels, local(): pl.pallas_call(functools.partial(finish_kernel, float(depth) ** (-0.5)),...  5.62 us

profile of v5, /device:TPU:4, one launch (start us, length us, event | category | flops | bytes accessed | tf_op | source)
XLA Modules:
  0.0 249.5 jit_solution(12060440813682043537)
XLA Ops:
  0.0 243.9 %exchange.1 = (f32[1024,2048]{1,0:T(8,128)S(1)}, bf16[1024,768]{1,0:T(8,128)(2,1)S(1)}, bf16[512,2048]{1,0:T(8,128)(2,1)S(1)}) custom-call(f32[2,2,1024,2048]{3,2,1,0:T(8,128)} %integrals_ref.1, s32[2,8,16]{2,1,0:T(8,128)} %mask_ref.1, f32[2048,640]{1,0:T(8,128)} %coeffs_ref.1), custom_call_target="tpu_custom_call" | custom-call | tf_op jit(solution)/shard_map/exchange/pallas_call | solution.py:425
  243.9 5.6 %finish.1 = f32[1024,2048]{1,0:T(8,128)} custom-call(f32[1024,2048]{1,0:T(8,128)S(1)} %get-tuple-element.8.acc_ref, bf16[1024,768]{1,0:T(8,128)(2,1)S(1)} %get-tuple-element.9.left_ref, bf16[512,2048]{1,0:T(8,128)(2,1)S(1)} %get-tuple-element.10.right_ref), custom_call_target="tpu_custom_call" | custom-call | tf_op jit(solution)/shard_map/finish/pallas_call | solution.py:457

commit v6 on v5

--- a/solution.py
+++ b/solution.py
@@ -398,9 +398,10 @@
 def finish_kernel(scale, acc_ref, left_ref, right_ref, out_ref):
     broad = out_ref.shape[1]
     at = pl.ds(pl.multiple_of(pl.program_id(0) * broad, broad), broad)
-    right = jnp.concatenate([right_ref[:, at], right_ref[:SPAN, at]], axis=0)
-    value = acc_ref[:, at] + jnp.dot(left_ref[...], right, preferred_element_type=jnp.float32)
-    out_ref[...] = value * scale
+    both, deep = left_ref[:, : 2 * SPAN], left_ref[:, 2 * SPAN :]
+    value = jnp.dot(both, right_ref[:, at], preferred_element_type=jnp.float32)
+    value = value + jnp.dot(deep, right_ref[:SPAN, at], preferred_element_type=jnp.float32)
+    out_ref[...] = (acc_ref[:, at] + value) * scale
 
 
 def local(loops, row_count, integrals, mask, coeffs):

time: 254 us -> 254 us (level)
  no operation moved by 1% of the time
where the time goes in v6:
time: 254 us; the launch traced here: 250 us
  Pallas kernels  250 us (98%)
    pallas_call x1, Pallas kernels, local(): pl.pallas_call(functools.partial(exchange_kernel, loops, row_count), out_...  244 us
    pallas_call x1, Pallas kernels, local(): pl.pallas_call(functools.partial(finish_kernel, float(depth) ** (-0.5)),...  5.62 us

profile of v6, /device:TPU:4, one launch (start us, length us, event | category | flops | bytes accessed | tf_op | source)
XLA Modules:
  0.0 249.5 jit_solution(5250058506800446240)
XLA Ops:
  0.0 243.9 %exchange.1 = (f32[1024,2048]{1,0:T(8,128)S(1)}, bf16[1024,768]{1,0:T(8,128)(2,1)S(1)}, bf16[512,2048]{1,0:T(8,128)(2,1)S(1)}) custom-call(f32[2,2,1024,2048]{3,2,1,0:T(8,128)} %integrals_ref.1, s32[2,8,16]{2,1,0:T(8,128)} %mask_ref.1, f32[2048,640]{1,0:T(8,128)} %coeffs_ref.1), custom_call_target="tpu_custom_call" | custom-call | tf_op jit(solution)/shard_map/exchange/pallas_call | solution.py:426
  243.9 5.6 %finish.1 = f32[1024,2048]{1,0:T(8,128)} custom-call(f32[1024,2048]{1,0:T(8,128)S(1)} %get-tuple-element.8.acc_ref, bf16[1024,768]{1,0:T(8,128)(2,1)S(1)} %get-tuple-element.9.left_ref, bf16[512,2048]{1,0:T(8,128)(2,1)S(1)} %get-tuple-element.10.right_ref), custom_call_target="tpu_custom_call" | custom-call | tf_op jit(solution)/shard_map/finish/pallas_call | solution.py:458
